TPU v7x, 256 devices: a whole 4x4x8 slice. The times are simulated.
256 devices in a mesh: grp: 2 (over z_lo), gx: 64 (over x, z_hi, y), gz: 2 (over core).
Axes of the slice: x: 4, y: 4, z: 8 (z_hi: 4, z_lo: 2; z = z_hi * 2 + z_lo), core: 2. Of those that a mesh axis runs over, the one named last changes fastest.
Arguments:
- fields: float32 [4, 2, 4, 4096, 1024], P(None, 'grp', None, 'gx', 'gz'), may hold values from -4 to 4
- buoyancy: float32 [2, 4, 4096, 1024], P('grp', None, 'gx', 'gz'), may hold values from 0.3 to 0.9
- stiffness: float32 [2, 4, 4096, 1024], P('grp', None, 'gx', 'gz'), may hold values from 0.2 to 0.7
- stress_zero: float32 [4096, 1024], P('gx', 'gz'), may hold values from -5 to 5
- direct_effect: float32 [4096, 1024], P('gx', 'gz'), may hold values from 1 to 8
- log_state: float32 [4096, 1024], P('gx', 'gz'), may hold values from -2 to 2
- kernel: float32 [16, 1024, 4096], P(None, ('grp', 'gx', 'gz')), may hold values from -2 to 2
- history: float32 [16, 1024, 2, 4096], P(None, ('grp', 'gx', 'gz')), may hold values from -5 to 5
- truncation: int32 [1024, 4096], P(('grp', 'gx', 'gz')), may hold values from 1 to 16
Outputs:
- fields_next: float32 [4, 2, 4, 4096, 1024], P(None, 'grp', None, 'gx', 'gz')
- state_next: float32 [4096, 1024], P('gx', 'gz')
- spectra_new: float32 [4, 1024, 2, 4096], P(None, ('grp', 'gx', 'gz'))
All inputs are finite; a program needn't handle non-finite values.
Results may differ from a plain program's by a relative error of at most 0.0003.
Values sent between devices are 32-bit elements; how exact they have to be, the bound alone decides.
A program may use at most 128 MiB of HBM per device.

v0:
```python
import math
import jax
import jax.numpy as jnp
from jax import lax
from jax.sharding import PartitionSpec as P

NSTEP = 4
NEWTON = 4
FACE_NEAR = 9.0 / 8.0
FACE_FAR = 1.0 / 24.0
DAMPING = 1.0
FULL_PRECISION = lax.Precision.HIGHEST


def extended(cells, sides, width):
    for axis, dim in sides:
        count = lax.axis_size(axis)
        ends = count - 1
        head = lax.slice_in_dim(cells, 0, width, axis=dim)
        tail = lax.slice_in_dim(cells, cells.shape[dim] - width, cells.shape[dim], axis=dim)
        cells = jnp.concatenate(
            [
                lax.ppermute(tail, axis, [(i, (i + 1) % count) for i in range(ends)]),
                cells,
                lax.ppermute(head, axis, [((i + 1) % count, i) for i in range(ends)]),
            ],
            axis=dim,
        )
    return cells


def from_partner(x, axis, stride):
    return lax.ppermute(x, axis, [(i, i ^ 1 << stride) for i in range(lax.axis_size(axis))])


def stencil(values, axis_index, pad_before, pad_after):
    widths = [(0, 0)] * values.ndim
    widths[axis_index] = (pad_before, pad_after)
    padded = jnp.pad(values, widths)
    length = values.shape[axis_index]

    def window(offset):
        return lax.slice_in_dim(padded, offset, offset + length, axis=axis_index)

    return FACE_NEAR * (window(2) - window(1)) - FACE_FAR * (window(3) - window(0))


def margin_stencil(padded, axis_index, length, lead_cells):

    def window(offset):
        return lax.slice_in_dim(
            padded, lead_cells + offset, lead_cells + offset + length, axis=axis_index
        )

    return FACE_NEAR * (window(2) - window(1)) - FACE_FAR * (window(3) - window(0))


def inverse_sinh(scaled):
    magnitude = jnp.abs(scaled)
    positive = jnp.log(magnitude + jnp.sqrt(1.0 + magnitude * magnitude))
    return jnp.where(scaled < 0.0, -positive, positive)


def friction(loading, direct_effect, log_state, initial):
    factor = jnp.exp(log_state)
    slip_rate = initial
    for repeat in range(NEWTON):
        scaled = slip_rate * factor
        misfit = direct_effect * inverse_sinh(scaled) + DAMPING * slip_rate - loading
        slope_total = direct_effect * factor / jnp.sqrt(1.0 + scaled * scaled) + DAMPING
        slip_rate = slip_rate - misfit / slope_total
    return slip_rate


def phase_table(first_index, second_index, length, direction):
    turn_count = first_index * second_index % length
    angle_value = turn_count.astype(jnp.float32) * (2.0 * math.pi / length)
    return (jnp.cos(angle_value), direction * jnp.sin(angle_value))


def complex_apply(real_part, imag_part, cos_table, sin_table, formula):
    real_cos = jnp.einsum(formula, real_part, cos_table, precision=FULL_PRECISION)
    imag_sin = jnp.einsum(formula, imag_part, sin_table, precision=FULL_PRECISION)
    real_sin = jnp.einsum(formula, real_part, sin_table, precision=FULL_PRECISION)
    imag_cos = jnp.einsum(formula, imag_part, cos_table, precision=FULL_PRECISION)
    return (real_cos - imag_sin, real_sin + imag_cos)


def strike_forward(values, outer_count, inner_count):
    planes_count = values.shape[0]
    total_count = outer_count * inner_count
    real_part = values[:, 0].reshape(planes_count, outer_count, inner_count)
    imag_part = values[:, 1].reshape(planes_count, outer_count, inner_count)
    outer_iota = jnp.arange(outer_count, dtype=jnp.int32)
    inner_iota = jnp.arange(inner_count, dtype=jnp.int32)
    cos_table, sin_table = phase_table(outer_iota[:, None], outer_iota[None, :], outer_count, -1.0)
    real_part, imag_part = complex_apply(real_part, imag_part, cos_table, sin_table, "rab,ak->rkb")
    cos_table, sin_table = phase_table(outer_iota[:, None], inner_iota[None, :], total_count, -1.0)
    real_part, imag_part = (
        real_part * cos_table - imag_part * sin_table,
        real_part * sin_table + imag_part * cos_table,
    )
    cos_table, sin_table = phase_table(inner_iota[:, None], inner_iota[None, :], inner_count, -1.0)
    real_part, imag_part = complex_apply(real_part, imag_part, cos_table, sin_table, "rkb,bm->rmk")
    return jnp.stack(
        [
            real_part.reshape(planes_count, total_count),
            imag_part.reshape(planes_count, total_count),
        ],
        axis=1,
    )


def strike_inverse(values, outer_count, inner_count):
    planes_count = values.shape[0]
    total_count = outer_count * inner_count
    real_part = values[:, 0].reshape(planes_count, inner_count, outer_count)
    imag_part = values[:, 1].reshape(planes_count, inner_count, outer_count)
    outer_iota = jnp.arange(outer_count, dtype=jnp.int32)
    inner_iota = jnp.arange(inner_count, dtype=jnp.int32)
    cos_table, sin_table = phase_table(inner_iota[:, None], inner_iota[None, :], inner_count, 1.0)
    real_part, imag_part = complex_apply(real_part, imag_part, cos_table, sin_table, "rmk,mb->rkb")
    cos_table, sin_table = phase_table(outer_iota[:, None], inner_iota[None, :], total_count, 1.0)
    real_part, imag_part = (
        real_part * cos_table - imag_part * sin_table,
        real_part * sin_table + imag_part * cos_table,
    )
    cos_table, sin_table = phase_table(outer_iota[:, None], outer_iota[None, :], outer_count, 1.0)
    real_part, imag_part = complex_apply(real_part, imag_part, cos_table, sin_table, "rkb,ka->rab")
    return jnp.stack(
        [
            real_part.reshape(planes_count, total_count),
            imag_part.reshape(planes_count, total_count),
        ],
        axis=1,
    )


def per_device(
    fields, buoyancy, stiffness, stress_zero, direct_effect, log_state, kernel, history, truncation
):
    side_index = lax.axis_index("grp")
    on_plus = side_index == 1
    depth_index = lax.axis_index("gz")
    strike_devices = lax.axis_size("gx")
    depth_devices = lax.axis_size("gz")
    velocity = fields[0]
    normal_stress = fields[1]
    shear_stress = fields[2:4]
    strike_rows = velocity.shape[2]
    depth_cols = velocity.shape[3]
    modes_dev = history.shape[1]
    strike_total = history.shape[3]
    depth_total = depth_cols * depth_devices
    mode_rows = strike_devices * modes_dev
    scale_back = 1.0 / math.sqrt(strike_total * depth_total)
    lag_number = lax.broadcasted_iota(jnp.int32, kernel.shape, 0)
    weights = jnp.where(lag_number < truncation[None], kernel, jnp.zeros_like(kernel))

    def mode_numbers(row_index, depth_part):
        return (
            (side_index * strike_devices + row_index // modes_dev) * depth_devices + depth_part
        ) * modes_dev + row_index % modes_dev

    own_modes = mode_numbers(jnp.arange(mode_rows, dtype=jnp.int32), depth_index)
    depth_iota = jnp.arange(depth_total, dtype=jnp.int32)
    back_cos, back_sin = phase_table(own_modes[:, None], depth_iota[None, :], depth_total, 1.0)
    lagged = history
    spectra = []
    for step_number in range(NSTEP):
        summed = jnp.sum(weights[:, :, None, :] * lagged, axis=0)
        in_space = strike_inverse(summed, strike_devices, strike_rows)
        by_rows = lax.all_to_all(in_space, "gx", split_axis=2, concat_axis=0, tiled=True)
        partial_value = jnp.einsum(
            "jy,jz->yz", by_rows[:, 0], back_cos, precision=FULL_PRECISION
        ) - jnp.einsum("jy,jz->yz", by_rows[:, 1], back_sin, precision=FULL_PRECISION)
        own_depth = lax.psum_scatter(partial_value, "gz", scatter_dimension=1, tiled=True)
        relief = lax.psum(own_depth, "grp") * scale_back
        padded = extended(velocity, (("gx", 2), ("gz", 3)), 2)
        normal_stress = normal_stress + stiffness * stencil(velocity, 1, 2, 1)
        strike_grad = margin_stencil(padded[:, :, :, 2 : 2 + depth_cols], 2, strike_rows, 1)
        depth_grad = margin_stencil(padded[:, :, 2 : 2 + strike_rows, :], 3, depth_cols, 1)
        shear_stress = shear_stress + stiffness * jnp.stack([strike_grad, depth_grad])
        near_plane = velocity[0, 0]
        far_plane = from_partner(near_plane, "grp", 0)
        velocity_plus = jnp.where(on_plus, near_plane, far_plane)
        velocity_minus = jnp.where(on_plus, far_plane, near_plane)
        slip_guess = velocity_plus - velocity_minus
        loading = stress_zero + relief + DAMPING * slip_guess
        slip_rate = friction(loading, direct_effect, log_state, slip_guess)
        traction = loading - DAMPING * slip_rate
        log_state = 0.75 * log_state - 0.2 * jnp.log(1.0 + slip_rate * slip_rate) + 0.1
        normal_stress = normal_stress.at[0, 0].set(jnp.where(on_plus, traction, -traction))
        shear_rim = extended(shear_stress, (("gx", 3), ("gz", 4)), 2)
        strike_div = margin_stencil(shear_rim[0][:, :, :, 2 : 2 + depth_cols], 2, strike_rows, 0)
        depth_div = margin_stencil(shear_rim[1][:, :, 2 : 2 + strike_rows, :], 3, depth_cols, 0)
        velocity = velocity + buoyancy * (stencil(normal_stress, 1, 1, 2) + strike_div + depth_div)
        term_index = jnp.arange(mode_rows * lax.axis_size("gz"), dtype=jnp.int32)
        term_modes = mode_numbers(term_index % mode_rows, term_index // mode_rows)
        depth_here = depth_index * depth_cols + jnp.arange(depth_cols, dtype=jnp.int32)
        cos_part, sin_part = phase_table(
            term_modes[:, None], depth_here[None, :], depth_total, -1.0
        )
        real_term = jnp.einsum("jz,yz->jy", cos_part, slip_rate, precision=FULL_PRECISION)
        imag_term = jnp.einsum("jz,yz->jy", sin_part, slip_rate, precision=FULL_PRECISION)
        by_modes = lax.psum_scatter(
            jnp.stack([real_term, imag_term], axis=1), "gz", scatter_dimension=0, tiled=True
        )
        spread = lax.all_to_all(by_modes, "gx", split_axis=0, concat_axis=2, tiled=True)
        fresh_modes = strike_forward(spread, strike_devices, strike_rows) * scale_back
        spectra.append(fresh_modes)
        lagged = jnp.concatenate([fresh_modes[None], lagged[:-1]], axis=0)
    return (
        jnp.stack([velocity, normal_stress, shear_stress[0], shear_stress[1]]),
        log_state,
        jnp.stack(spectra),
    )


def solution(mesh):
    return jax.shard_map(
        per_device,
        mesh=mesh,
        in_specs=(
            P(None, "grp", None, "gx", "gz"),
            P("grp", None, "gx", "gz"),
            P("grp", None, "gx", "gz"),
            P("gx", "gz"),
            P("gx", "gz"),
            P("gx", "gz"),
            P(None, ("grp", "gx", "gz"), None),
            P(None, ("grp", "gx", "gz"), None, None),
            P(("grp", "gx", "gz"), None),
        ),
        out_specs=(
            P(None, "grp", None, "gx", "gz"),
            P("gx", "gz"),
            P(None, ("grp", "gx", "gz"), None, None),
        ),
        check_vma=False,
    )
```

profile of v0, /device:TPU:1, one launch (start us, length us, event | category | flops | bytes accessed | tf_op | source)
XLA Modules:
  0.0 803.6 jit_solution(6997939394833421156)
XLA Ops:
  26.4 7.4 reshape.589
  33.9 18.6 %all-to-all-start = ((f32[64,1,512]{2,1,0:T(1,128)}), f32[64,1,512]{2,1,0:T(1,128)S(1)}, u32[]{:S(2)}, u32[]{:S(2)}) async-start(f32[64,1,512]{2,1,0:T(1,128)} %reshape.589), calls=%async_computation | async-start | bytes 262144 | tf_op jit(solution)/shard_map/all_to_all | solution.py:173
  69.9 7.9 reshape.590
  94.1 10.1 %collective-permute-start = (f32[64,512]{1,0:T(8,128)}, f32[64,512]{1,0:T(8,128)}, u32[]{:S(2)}, u32[]{:S(2)}) collective-permute-start(f32[64,512]{1,0:T(8,128)} %slice_bitcast_fusion.24), channel_id=1, source_target_pairs={{0,128},{128,0},{1,129},{129,1},{2,130},{130,2},{3,131},{131,3},{4... | collective-permute-start | bytes 393224 | tf_op jit(solution)/shard_map/ppermute | solution.py:33
  117.8 33.4 %all-reduce.13.cloned.1.call-done = f32[64,512]{1,0:T(8,128)} async-done(((f32[64,512]{1,0:T(8,128)}), f32[64,512]{1,0:T(8,128)}) %all-reduce.13.cloned.1.call-update) | async-done | bytes 131088 | tf_op jit(solution)/shard_map/psum | solution.py:178
  187.7 17.2 %all-to-all-start.1 = ((f32[64,1,512]{2,1,0:T(1,128)}), f32[64,1,512]{2,1,0:T(1,128)S(1)}, u32[]{:S(2)}, u32[]{:S(2)}) async-start(f32[64,1,512]{2,1,0:T(1,128)} %reshape.591), calls=%async_computation.3 | async-start | bytes 262144 | tf_op jit(solution)/shard_map/all_to_all | solution.py:209
  208.3 8.1 %all-to-all-done.1 = f32[64,1,512]{2,1,0:T(1,128)S(1)} async-done(((f32[64,1,512]{2,1,0:T(1,128)}), f32[64,1,512]{2,1,0:T(1,128)S(1)}, u32[]{:S(2)}, u32[]{:S(2)}) %all-to-all-start.1) | async-done | bytes 131104 | tf_op jit(solution)/shard_map/all_to_all | solution.py:209
  260.6 7.4 reshape.593
  285.0 8.0 reshape.594
  328.1 32.7 %all-reduce.15.cloned.1.call-done = f32[64,512]{1,0:T(8,128)} async-done(((f32[64,512]{1,0:T(8,128)}), f32[64,512]{1,0:T(8,128)}) %all-reduce.15.cloned.1.call-update) | async-done | bytes 131088 | tf_op jit(solution)/shard_map/psum | solution.py:178
  391.2 7.4 reduce-scatter.15.cloned.1.call-done
  402.2 12.6 %all-to-all-start.3 = ((f32[64,1,512]{2,1,0:T(1,128)}), f32[64,1,512]{2,1,0:T(1,128)}, u32[]{:S(2)}, u32[]{:S(2)}) async-start(f32[64,1,512]{2,1,0:T(1,128)} %reshape.595), calls=%async_computation.7 | async-start | bytes 262144 | tf_op jit(solution)/shard_map/all_to_all | solution.py:209
  418.1 8.6 %all-to-all-done.3 = f32[64,1,512]{2,1,0:T(1,128)} async-done(((f32[64,1,512]{2,1,0:T(1,128)}), f32[64,1,512]{2,1,0:T(1,128)}, u32[]{:S(2)}, u32[]{:S(2)}) %all-to-all-start.3) | async-done | bytes 131104 | tf_op jit(solution)/shard_map/all_to_all | solution.py:209
  454.8 7.5 reshape.597
  480.8 8.3 %reshape.598 = f32[4096,2,4]{2,1,0:T(2,128)} reshape(f32[64,512]{1,0:T(8,128)S(1)} %reduce.44) | data formatting | bytes 262144
  523.7 32.8 %all-reduce.17.cloned.1.call-done = f32[64,512]{1,0:T(8,128)} async-done(((f32[64,512]{1,0:T(8,128)}), f32[64,512]{1,0:T(8,128)}) %all-reduce.17.cloned.1.call-update) | async-done | bytes 131088 | tf_op jit(solution)/shard_map/psum | solution.py:178
  588.4 17.2 %all-to-all-start.5 = ((f32[64,1,512]{2,1,0:T(1,128)}), f32[64,1,512]{2,1,0:T(1,128)S(1)}, u32[]{:S(2)}, u32[]{:S(2)}) async-start(f32[64,1,512]{2,1,0:T(1,128)} %reshape.599), calls=%async_computation.11 | async-start | bytes 262144 | tf_op jit(solution)/shard_map/all_to_all | solution.py:209
  639.7 7.5 reshape.601
  647.2 6.9 all-to-all-start.6
  656.8 8.7 %all-to-all-done.6 = f32[64,1,512]{2,1,0:T(1,128)S(1)} async-done(((f32[64,1,512]{2,1,0:T(1,128)}), f32[64,1,512]{2,1,0:T(1,128)S(1)}, u32[]{:S(2)}, u32[]{:S(2)}) %all-to-all-start.6) | async-done | bytes 131104 | tf_op jit(solution)/shard_map/all_to_all | solution.py:173
  666.5 7.9 reshape.602
  709.1 25.8 %all-reduce.19.cloned.1.call-done = f32[64,512]{1,0:T(8,128)} async-done(((f32[64,512]{1,0:T(8,128)}), f32[64,512]{1,0:T(8,128)}) %all-reduce.19.cloned.1.call-update) | async-done | bytes 131088 | tf_op jit(solution)/shard_map/psum | solution.py:178
  750.1 12.4 %reduce-scatter.23.cloned.1.call-done = f32[256,2,64]{0,2,1:T(8,128)} async-done(((f32[512,2,64]{0,2,1:T(8,128)}), f32[256,2,64]{0,2,1:T(8,128)}) %reduce-scatter.23.cloned.1.call-update) | async-done | bytes 131088 | tf_op jit(solution)/shard_map/reduce_scatter | solution.py:206
  764.5 12.3 %all-to-all-start.7 = ((f32[64,1,512]{2,1,0:T(1,128)}), f32[64,1,512]{2,1,0:T(1,128)S(1)}, u32[]{:S(2)}, u32[]{:S(2)}) async-start(f32[64,1,512]{2,1,0:T(1,128)} %reshape.603), calls=%async_computation.15 | async-start | bytes 262144 | tf_op jit(solution)/shard_map/all_to_all | solution.py:209
  (453 shorter events, 460.5 us)
Async XLA Ops:
  8.4 44.1 %collective-permute-start.1 = (f32[1,4,2,512]{3,2,1,0:T(2,128)S(1)}, f32[1,4,2,512]{3,2,1,0:T(2,128)S(1)}, u32[]{:S(2)}, u32[]{:S(2)}) collective-permute-start(f32[1,4,2,512]{3,2,1,0:T(2,128)S(1)} %get-tuple-element.127), channel_id=1, source_target_pairs={{2,0},{4,2},{6,4},{8,6},{10,8},{12,10},{14,12},{16,14},{18,16},{20... | collective-permute-start | bytes 49160 | tf_op jit(solution)/shard_map/ppermute | solution.py:25
  9.7 42.8 %collective-permute-start.2 = (f32[1,4,2,512]{3,2,1,0:T(2,128)S(1)}, f32[1,4,2,512]{3,2,1,0:T(2,128)S(1)}, u32[]{:S(2)}, u32[]{:S(2)}) collective-permute-start(f32[1,4,2,512]{3,2,1,0:T(2,128)S(1)} %get-tuple-element.126), channel_id=1, source_target_pairs={{0,2},{2,4},{4,6},{6,8},{8,10},{10,12},{12,14},{14,16},{16,18},{18... | collective-permute-start | bytes 49160 | tf_op jit(solution)/shard_map/ppermute | solution.py:23
  33.9 34.6 %all-to-all-start = ((f32[64,1,512]{2,1,0:T(1,128)}), f32[64,1,512]{2,1,0:T(1,128)S(1)}, u32[]{:S(2)}, u32[]{:S(2)}) async-start(f32[64,1,512]{2,1,0:T(1,128)} %reshape.589), calls=%async_computation | async-start | bytes 262144 | tf_op jit(solution)/shard_map/all_to_all | solution.py:173
  52.5 62.6 %reduce-scatter.9.cloned.1.call-start = ((), (), s32[]{:S(2)}) async-start(), calls=%async_computation.16 | async-start | bytes 393216 | tf_op jit(solution)/shard_map/reduce_scatter | solution.py:177
  63.7 40.4 %collective-permute-start.5 = (f32[2,1,4,2,512]{4,3,2,1,0:T(2,128)}, f32[2,1,4,2,512]{4,3,2,1,0:T(2,128)S(1)}, u32[]{:S(2)}, u32[]{:S(2)}) collective-permute-start(f32[2,1,4,2,512]{4,3,2,1,0:T(2,128)} %get-tuple-element.98), channel_id=1, source_target_pairs={{0,2},{2,4},{4,6},{6,8},{8,10},{10,12},{12,14},{14,16},{16,18},{18... | collective-permute-start | bytes 98312 | tf_op jit(solution)/shard_map/ppermute | solution.py:23
  66.9 37.2 %collective-permute-start.6 = (f32[2,1,4,2,512]{4,3,2,1,0:T(2,128)}, f32[2,1,4,2,512]{4,3,2,1,0:T(2,128)S(1)}, u32[]{:S(2)}, u32[]{:S(2)}) collective-permute-start(f32[2,1,4,2,512]{4,3,2,1,0:T(2,128)} %get-tuple-element.99), channel_id=1, source_target_pairs={{2,0},{4,2},{6,4},{8,6},{10,8},{12,10},{14,12},{16,14},{18,16},{20... | collective-permute-start | bytes 98312 | tf_op jit(solution)/shard_map/ppermute | solution.py:25
  93.4 57.8 %all-reduce.13.cloned.1.call-start = ((), (), s32[]{:S(2)}) async-start(), calls=%async_computation.17 | async-start | bytes 262144 | tf_op jit(solution)/shard_map/psum | solution.py:178
  115.2 70.6 %reduce-scatter.11.cloned.1.call-start = ((), (), s32[]{:S(2)}) async-start(), calls=%async_computation.18 | async-start | bytes 393216 | tf_op jit(solution)/shard_map/reduce_scatter | solution.py:206
  272.6 52.8 %reduce-scatter.13.cloned.1.call-start = ((), (), s32[]{:S(2)}) async-start(), calls=%async_computation.19 | async-start | bytes 393216 | tf_op jit(solution)/shard_map/reduce_scatter | solution.py:177
  275.7 32.9 %collective-permute-start.14 = (f32[2,1,4,2,512]{4,3,2,1,0:T(2,128)S(1)}, f32[2,1,4,2,512]{4,3,2,1,0:T(2,128)S(1)}, u32[]{:S(2)}, u32[]{:S(2)}) collective-permute-start(f32[2,1,4,2,512]{4,3,2,1,0:T(2,128)S(1)} %get-tuple-element.96), channel_id=1, source_target_pairs={{0,2},{2,4},{4,6},{6,8},{8,10},{10,12},{12,14},{14,16},{16,18},{18... | collective-permute-start | bytes 98312 | tf_op jit(solution)/shard_map/ppermute | solution.py:23
  278.5 30.1 %collective-permute-start.15 = (f32[2,1,4,2,512]{4,3,2,1,0:T(2,128)S(1)}, f32[2,1,4,2,512]{4,3,2,1,0:T(2,128)S(1)}, u32[]{:S(2)}, u32[]{:S(2)}) collective-permute-start(f32[2,1,4,2,512]{4,3,2,1,0:T(2,128)S(1)} %get-tuple-element.97), channel_id=1, source_target_pairs={{2,0},{4,2},{6,4},{8,6},{10,8},{12,10},{14,12},{16,14},{18,16},{20... | collective-permute-start | bytes 98312 | tf_op jit(solution)/shard_map/ppermute | solution.py:25
  308.5 52.2 %all-reduce.15.cloned.1.call-start = ((), (), s32[]{:S(2)}) async-start(), calls=%async_computation.20 | async-start | bytes 262144 | tf_op jit(solution)/shard_map/psum | solution.py:178
  325.5 73.1 %reduce-scatter.15.cloned.1.call-start = ((), (), s32[]{:S(2)}) async-start(), calls=%async_computation.21 | async-start | bytes 393216 | tf_op jit(solution)/shard_map/reduce_scatter | solution.py:206
  467.7 53.3 %reduce-scatter.17.cloned.1.call-start = ((), (), s32[]{:S(2)}) async-start(), calls=%async_computation.22 | async-start | bytes 393216 | tf_op jit(solution)/shard_map/reduce_scatter | solution.py:177
  471.8 32.9 %collective-permute-start.23 = (f32[2,1,4,2,512]{4,3,2,1,0:T(2,128)}, f32[2,1,4,2,512]{4,3,2,1,0:T(2,128)S(1)}, u32[]{:S(2)}, u32[]{:S(2)}) collective-permute-start(f32[2,1,4,2,512]{4,3,2,1,0:T(2,128)} %get-tuple-element.94), channel_id=1, source_target_pairs={{0,2},{2,4},{4,6},{6,8},{8,10},{10,12},{12,14},{14,16},{16,18},{18... | collective-permute-start | bytes 98312 | tf_op jit(solution)/shard_map/ppermute | solution.py:23
  474.6 30.2 %collective-permute-start.24 = (f32[2,1,4,2,512]{4,3,2,1,0:T(2,128)}, f32[2,1,4,2,512]{4,3,2,1,0:T(2,128)}, u32[]{:S(2)}, u32[]{:S(2)}) collective-permute-start(f32[2,1,4,2,512]{4,3,2,1,0:T(2,128)} %get-tuple-element.95), channel_id=1, source_target_pairs={{2,0},{4,2},{6,4},{8,6},{10,8},{12,10},{14,12},{16,14},{18,16},{20... | collective-permute-start | bytes 98312 | tf_op jit(solution)/shard_map/ppermute | solution.py:25
  504.7 51.8 %all-reduce.17.cloned.1.call-start = ((), (), s32[]{:S(2)}) async-start(), calls=%async_computation.23 | async-start | bytes 262144 | tf_op jit(solution)/shard_map/psum | solution.py:178
  521.1 65.3 %reduce-scatter.19.cloned.1.call-start = ((), (), s32[]{:S(2)}) async-start(), calls=%async_computation.24 | async-start | bytes 393216 | tf_op jit(solution)/shard_map/reduce_scatter | solution.py:206
  609.2 45.0 %collective-permute-start.31 = (f32[1,4,68,2]{3,2,1,0:T(8,128)}, f32[1,4,68,2]{3,2,1,0:T(8,128)}, u32[]{:S(2)}, u32[]{:S(2)}) collective-permute-start(f32[1,4,68,2]{3,2,1,0:T(8,128)} %get-tuple-element.103), channel_id=1, source_target_pairs={{0,1},{2,3},{4,5},{6,7},{8,9},{10,11},{12,13},{14,15},{16,17},{18,... | collective-permute-start | bytes 6536 | tf_op jit(solution)/shard_map/ppermute | solution.py:23
  654.1 45.3 %reduce-scatter.21.cloned.1.call-start = ((), (), s32[]{:S(2)}) async-start(), calls=%async_computation.25 | async-start | bytes 393216 | tf_op jit(solution)/shard_map/reduce_scatter | solution.py:177
  690.0 44.9 %all-reduce.19.cloned.1.call-start = ((), (), s32[]{:S(2)}) async-start(), calls=%async_computation.26 | async-start | bytes 262144 | tf_op jit(solution)/shard_map/psum | solution.py:178
  699.5 63.0 %reduce-scatter.23.cloned.1.call-start = ((), (), s32[]{:S(2)}) async-start(), calls=%async_computation.27 | async-start | bytes 393216 | tf_op jit(solution)/shard_map/reduce_scatter | solution.py:206
  701.2 46.5 %collective-permute-start.34 = (f32[2,1,4,68,2]{4,3,2,1,0:T(8,128)}, f32[2,1,4,68,2]{4,3,2,1,0:T(8,128)S(1)}, u32[]{:S(2)}, u32[]{:S(2)}) collective-permute-start(f32[2,1,4,68,2]{4,3,2,1,0:T(8,128)} %get-tuple-element.84), channel_id=1, source_target_pairs={{0,1},{2,3},{4,5},{6,7},{8,9},{10,11},{12,13},{14,15},{16,17},{18,... | collective-permute-start | bytes 13064 | tf_op jit(solution)/shard_map/ppermute | solution.py:23
  702.5 45.2 %collective-permute-start.35 = (f32[2,1,4,68,2]{4,3,2,1,0:T(8,128)}, f32[2,1,4,68,2]{4,3,2,1,0:T(8,128)S(1)}, u32[]{:S(2)}, u32[]{:S(2)}) collective-permute-start(f32[2,1,4,68,2]{4,3,2,1,0:T(8,128)} %get-tuple-element.85), channel_id=1, source_target_pairs={{1,0},{3,2},{5,4},{7,6},{9,8},{11,10},{13,12},{15,14},{17,16},{19,... | collective-permute-start | bytes 13064 | tf_op jit(solution)/shard_map/ppermute | solution.py:25
  (82 other events, 1418.4 us)
Sparse Core Ops, SparseCore 0:
  93.5 17.6 reduce-scatter.8
  115.3 35.8 all-reduce.12
  164.1 14.6 reduce-scatter.10
  308.6 16.7 reduce-scatter.12
  327.8 32.8 all-reduce.14
  380.1 18.4 reduce-scatter.14
  504.8 16.1 reduce-scatter.16
  523.6 32.8 all-reduce.16
  569.5 14.6 reduce-scatter.18
  690.1 9.2 reduce-scatter.20
  702.0 32.8 all-reduce.18
  747.8 14.6 reduce-scatter.22
where the time goes:
time: 815 us; the launch traced here: 804 us
  waiting for transfers between devices  205 us (25%)
  starting transfers between devices  197 us (24%)
  local copies, waits for them, and re-layouts  159 us (20%)
  matrix products  123 us (15%)
  other arithmetic  104 us (13%)
  between operations  16.4 us (2%)
    psum x4, waiting for transfers between devices, per_device(): relief = lax.psum(own_depth, 'grp') * scale_back  125 us
    unnamed x116, local copies, waits for them, and re-layouts  73.8 us
    all_to_all x4, starting transfers between devices, per_device(): lax.all_to_all(by_modes, 'gx', split_axis=0, concat_axis=2, tiled=True)  59.3 us
    ppermute x16, starting transfers between devices, extended(): lax.ppermute(head, axis, [((i + 1) % count, i) for i in range(ends)])  50.3 us
    ppermute x16, starting transfers between devices, extended(): lax.ppermute(tail, axis, [(i, (i + 1) % count) for i in range(ends)])  38.2 us
    all_to_all x4, starting transfers between devices, per_device(): lax.all_to_all(in_space, 'gx', split_axis=2, concat_axis=0, tiled=True)  35.7 us
    all_to_all x4, waiting for transfers between devices, per_device(): lax.all_to_all(by_modes, 'gx', split_axis=0, concat_axis=2, tiled=True)  27.6 us
    all_to_all x9, local copies, waits for them, and re-layouts, per_device(): lax.all_to_all(in_space, 'gx', split_axis=2, concat_axis=0, tiled=True)  22.7 us
  transfers between devices with their start and end apart: 56, of which 22 were waited for; matrix products, arithmetic and copies ran while one was open for 28% of the time, Pallas kernels for 0%

commit v1 on v0

--- a/solution.py
+++ b/solution.py
@@ -3,6 +3,7 @@
 import jax.numpy as jnp
 from jax import lax
 from jax.sharding import PartitionSpec as P
+from jax.lax import all_gather
 
 NSTEP = 4
 NEWTON = 4
@@ -10,6 +11,10 @@
 FACE_FAR = 1.0 / 24.0
 DAMPING = 1.0
 FULL_PRECISION = lax.Precision.HIGHEST
+
+
+def get_joints(state, lane_axis):
+    return jnp.sum(all_gather(state, lane_axis), 0)
 
 
 def extended(cells, sides, width):
@@ -175,7 +180,7 @@
             "jy,jz->yz", by_rows[:, 0], back_cos, precision=FULL_PRECISION
         ) - jnp.einsum("jy,jz->yz", by_rows[:, 1], back_sin, precision=FULL_PRECISION)
         own_depth = lax.psum_scatter(partial_value, "gz", scatter_dimension=1, tiled=True)
-        relief = lax.psum(own_depth, "grp") * scale_back
+        relief = get_joints(own_depth, "grp") * scale_back
         padded = extended(velocity, (("gx", 2), ("gz", 3)), 2)
         normal_stress = normal_stress + stiffness * stencil(velocity, 1, 2, 1)
         strike_grad = margin_stencil(padded[:, :, :, 2 : 2 + depth_cols], 2, strike_rows, 1)

time: 815 us -> 740 us (0.908)
  waiting for transfers between devices: 205 us -> 137 us
  blocking collectives: 0 us -> 37.9 us
  starting transfers between devices: 197 us -> 175 us
  matrix products: 123 us -> 111 us
    psum x4 -> x0, waiting for transfers between devices: 125 us -> none  [per_device(): relief = lax.psum(own_depth, 'grp') * scale_back]
    reduce_scatter x4, waiting for transfers between devices: 11 us -> 51 us  [per_device(): lax.psum_scatter(partial_value, 'gz', scatter_dimension=1, tiled=True)]
    all_gather x0 -> x4, blocking collectives: none -> 37.9 us  [get_joints(): return jnp.sum(all_gather(state, lane_axis), 0)]
    ppermute x16, waiting for transfers between devices: 1.57 us -> 12.7 us  [extended(): lax.ppermute(head, axis, [((i + 1) % count, i) for i in range(ends)])]
    ppermute x4, starting transfers between devices: 12.7 us -> 3.45 us  [from_partner(): lax.ppermute(x, axis, [(i, i ^ 1 << stride) for i in range(lax.axis_size(...]
    reduce_scatter x4, waiting for transfers between devices: 19.8 us -> 28.7 us  [per_device(): lax.psum_scatter(jnp.stack([real_term, imag_term], axis=1), 'gz', scatter...]
    unnamed x116 -> x122, local copies, waits for them, and re-layouts: 73.8 us -> 70.3 us
  transfers between devices with their start and end apart: 56 -> 52, of which waited for: 22 -> 22; matrix products, arithmetic and copies ran while one was open for 28% -> 22% of each run, Pallas kernels for 0% -> 0%
where the time goes in v1:
time: 740 us; the launch traced here: 728 us
  starting transfers between devices  175 us (24%)
  local copies, waits for them, and re-layouts  151 us (20%)
  waiting for transfers between devices  137 us (19%)
  matrix products  111 us (15%)
  other arithmetic  98.7 us (13%)
  blocking collectives  37.9 us (5%)
  between operations  16.6 us (2%)
    unnamed x122, local copies, waits for them, and re-layouts  70.3 us
    all_to_all x4, starting transfers between devices, per_device(): lax.all_to_all(by_modes, 'gx', split_axis=0, concat_axis=2, tiled=True)  53.3 us
    reduce_scatter x4, waiting for transfers between devices, per_device(): lax.psum_scatter(partial_value, 'gz', scatter_dimension=1, tiled=True)  51 us
    ppermute x16, starting transfers between devices, extended(): lax.ppermute(head, axis, [((i + 1) % count, i) for i in range(ends)])  49.8 us
    ppermute x16, starting transfers between devices, extended(): lax.ppermute(tail, axis, [(i, (i + 1) % count) for i in range(ends)])  38.3 us
    all_gather x4, blocking collectives, get_joints(): return jnp.sum(all_gather(state, lane_axis), 0)  37.9 us
    all_to_all x4, waiting for transfers between devices, per_device(): lax.all_to_all(by_modes, 'gx', split_axis=0, concat_axis=2, tiled=True)  31.6 us
    all_to_all x4, starting transfers between devices, per_device(): lax.all_to_all(in_space, 'gx', split_axis=2, concat_axis=0, tiled=True)  30.1 us
  transfers between devices with their start and end apart: 52, of which 22 were waited for; matrix products, arithmetic and copies ran while one was open for 22% of the time, Pallas kernels for 0%

profile of v1, /device:TPU:1, one launch (start us, length us, event | category | flops | bytes accessed | tf_op | source)
XLA Modules:
  0.0 728.1 jit_solution(5505913111794437823)
XLA Ops:
  19.3 7.4 %reshape.593 = f32[64,1,512]{2,1,0:T(1,128)} reshape(f32[4096,2,4]{2,1,0:T(2,128)} %bitcast.433) | data formatting | bytes 262144
  26.7 15.2 %all-to-all-start = ((f32[64,1,512]{2,1,0:T(1,128)}), f32[64,1,512]{2,1,0:T(1,128)S(1)}, u32[]{:S(2)}, u32[]{:S(2)}) async-start(f32[64,1,512]{2,1,0:T(1,128)} %reshape.593), calls=%async_computation | async-start | bytes 262144 | tf_op jit(solution)/shard_map/all_to_all | solution.py:178
  78.6 7.8 %reshape.594 = f32[4096,2,4]{2,1,0:T(2,128)} reshape(f32[64,512]{1,0:T(8,128)S(1)} %reduce.40) | data formatting | bytes 262144
  105.4 25.0 %reduce-scatter.9.cloned.1.call-done = f32[64,512]{1,0:T(8,128)} async-done(((f32[64,1024]{1,0:T(8,128)}), f32[64,512]{1,0:T(8,128)}) %reduce-scatter.9.cloned.1.call-update) | async-done | bytes 131088 | tf_op jit(solution)/shard_map/reduce_scatter | solution.py:182
  130.4 17.4 %all-gather = f32[128,512]{1,0:T(8,128)} all-gather(f32[64,512]{1,0:T(8,128)} %reduce-scatter.9.cloned.1.call-done), channel_id=2, replica_groups=mesh['grp'=2,'gx'=64,'gz'=2] {'grp'}, dimensions={0}, use_global_device_ids=true | all-gather | bytes 393216 | tf_op jit(solution)/shard_map/all_gather | solution.py:17
  191.6 15.3 %all-to-all-start.1 = ((f32[64,1,512]{2,1,0:T(1,128)}), f32[64,1,512]{2,1,0:T(1,128)S(1)}, u32[]{:S(2)}, u32[]{:S(2)}) async-start(f32[64,1,512]{2,1,0:T(1,128)} %reshape.595), calls=%async_computation.3 | async-start | bytes 262144 | tf_op jit(solution)/shard_map/all_to_all | solution.py:214
  209.9 9.0 %all-to-all-done.1 = f32[64,1,512]{2,1,0:T(1,128)S(1)} async-done(((f32[64,1,512]{2,1,0:T(1,128)}), f32[64,1,512]{2,1,0:T(1,128)S(1)}, u32[]{:S(2)}, u32[]{:S(2)}) %all-to-all-start.1) | async-done | bytes 131104 | tf_op jit(solution)/shard_map/all_to_all | solution.py:214
  242.4 7.4 %reshape.597 = f32[64,1,512]{2,1,0:T(1,128)} reshape(f32[4096,2,4]{2,1,0:T(2,128)} %bitcast.435) | data formatting | bytes 262144
  273.9 7.8 %reshape.598 = f32[4096,2,4]{2,1,0:T(2,128)} reshape(f32[64,512]{1,0:T(8,128)S(1)} %reduce.42) | data formatting | bytes 262144
  302.4 12.9 %reduce-scatter.13.cloned.1.call-done = f32[64,512]{1,0:T(8,128)} async-done(((f32[64,1024]{1,0:T(8,128)}), f32[64,512]{1,0:T(8,128)}) %reduce-scatter.13.cloned.1.call-update) | async-done | bytes 131088 | tf_op jit(solution)/shard_map/reduce_scatter | solution.py:182
  315.3 7.2 all-gather.1
  364.6 12.8 %all-to-all-start.3 = ((f32[64,1,512]{2,1,0:T(1,128)}), f32[64,1,512]{2,1,0:T(1,128)}, u32[]{:S(2)}, u32[]{:S(2)}) async-start(f32[64,1,512]{2,1,0:T(1,128)} %reshape.599), calls=%async_computation.7 | async-start | bytes 262144 | tf_op jit(solution)/shard_map/all_to_all | solution.py:214
  380.8 8.5 %all-to-all-done.3 = f32[64,1,512]{2,1,0:T(1,128)} async-done(((f32[64,1,512]{2,1,0:T(1,128)}), f32[64,1,512]{2,1,0:T(1,128)}, u32[]{:S(2)}, u32[]{:S(2)}) %all-to-all-start.3) | async-done | bytes 131104 | tf_op jit(solution)/shard_map/all_to_all | solution.py:214
  417.2 7.4 %reshape.601 = f32[64,1,512]{2,1,0:T(1,128)} reshape(f32[4096,2,4]{2,1,0:T(2,128)} %bitcast.437) | data formatting | bytes 262144
  448.7 7.8 %reshape.602 = f32[4096,2,4]{2,1,0:T(2,128)} reshape(f32[64,512]{1,0:T(8,128)S(1)} %reduce.44) | data formatting | bytes 262144
  477.0 13.1 %reduce-scatter.17.cloned.1.call-done = f32[64,512]{1,0:T(8,128)} async-done(((f32[64,1024]{1,0:T(8,128)}), f32[64,512]{1,0:T(8,128)}) %reduce-scatter.17.cloned.1.call-update) | async-done | bytes 131088 | tf_op jit(solution)/shard_map/reduce_scatter | solution.py:182
  490.1 7.3 all-gather.2
  540.1 12.6 %all-to-all-start.5 = ((f32[64,1,512]{2,1,0:T(1,128)}), f32[64,1,512]{2,1,0:T(1,128)}, u32[]{:S(2)}, u32[]{:S(2)}) async-start(f32[64,1,512]{2,1,0:T(1,128)} %reshape.603), calls=%async_computation.11 | async-start | bytes 262144 | tf_op jit(solution)/shard_map/all_to_all | solution.py:214
  556.0 8.6 %all-to-all-done.5 = f32[64,1,512]{2,1,0:T(1,128)} async-done(((f32[64,1,512]{2,1,0:T(1,128)}), f32[64,1,512]{2,1,0:T(1,128)}, u32[]{:S(2)}, u32[]{:S(2)}) %all-to-all-start.5) | async-done | bytes 131104 | tf_op jit(solution)/shard_map/all_to_all | solution.py:214
  587.5 7.6 %reshape.605 = f32[64,1,512]{2,1,0:T(1,128)} reshape(f32[4096,2,4]{2,1,0:T(2,128)} %bitcast.439) | data formatting | bytes 262144
  603.6 8.3 %all-to-all-done.6 = f32[64,1,512]{2,1,0:T(1,128)} async-done(((f32[64,1,512]{2,1,0:T(1,128)}), f32[64,1,512]{2,1,0:T(1,128)}, u32[]{:S(2)}, u32[]{:S(2)}) %all-to-all-start.6) | async-done | bytes 131104 | tf_op jit(solution)/shard_map/all_to_all | solution.py:178
  613.7 7.8 %reshape.606 = f32[4096,2,4]{2,1,0:T(2,128)} reshape(f32[64,512]{1,0:T(8,128)S(1)} %reduce.46) | data formatting | bytes 262144
  672.9 13.8 %reduce-scatter.23.cloned.1.call-done = f32[256,2,64]{0,2,1:T(8,128)} async-done(((f32[512,2,64]{0,2,1:T(8,128)}), f32[256,2,64]{0,2,1:T(8,128)}) %reduce-scatter.23.cloned.1.call-update) | async-done | bytes 131088 | tf_op jit(solution)/shard_map/reduce_scatter | solution.py:211
  688.8 12.6 %all-to-all-start.7 = ((f32[64,1,512]{2,1,0:T(1,128)}), f32[64,1,512]{2,1,0:T(1,128)S(1)}, u32[]{:S(2)}, u32[]{:S(2)}) async-start(f32[64,1,512]{2,1,0:T(1,128)} %reshape.607), calls=%async_computation.15 | async-start | bytes 262144 | tf_op jit(solution)/shard_map/all_to_all | solution.py:214
  (456 shorter events, 450.6 us)
Async XLA Ops:
  26.7 50.4 %all-to-all-start = ((f32[64,1,512]{2,1,0:T(1,128)}), f32[64,1,512]{2,1,0:T(1,128)S(1)}, u32[]{:S(2)}, u32[]{:S(2)}) async-start(f32[64,1,512]{2,1,0:T(1,128)} %reshape.593), calls=%async_computation | async-start | bytes 262144 | tf_op jit(solution)/shard_map/all_to_all | solution.py:178
  41.9 88.5 %reduce-scatter.9.cloned.1.call-start = ((), (), s32[]{:S(2)}) async-start(), calls=%async_computation.16 | async-start | bytes 393216 | tf_op jit(solution)/shard_map/reduce_scatter | solution.py:182
  49.1 100.4 %collective-permute-start = (f32[64,512]{1,0:T(8,128)}, f32[64,512]{1,0:T(8,128)}, u32[]{:S(2)}, u32[]{:S(2)}) collective-permute-start(f32[64,512]{1,0:T(8,128)} %slice_bitcast_fusion.24), channel_id=1, source_target_pairs={{0,128},{128,0},{1,129},{129,1},{2,130},{130,2},{3,131},{131,3},{4... | collective-permute-start | bytes 393224 | tf_op jit(solution)/shard_map/ppermute | solution.py:38
  70.9 31.2 %collective-permute-start.7 = (f32[2,1,4,68,2]{4,3,2,1,0:T(8,128)}, f32[2,1,4,68,2]{4,3,2,1,0:T(8,128)}, u32[]{:S(2)}, u32[]{:S(2)}) collective-permute-start(f32[2,1,4,68,2]{4,3,2,1,0:T(8,128)} %get-tuple-element.90), channel_id=1, source_target_pairs={{0,1},{2,3},{4,5},{6,7},{8,9},{10,11},{12,13},{14,15},{16,17},{18,... | collective-permute-start | bytes 13064 | tf_op jit(solution)/shard_map/ppermute | solution.py:28
  72.2 29.9 %collective-permute-start.8 = (f32[2,1,4,68,2]{4,3,2,1,0:T(8,128)}, f32[2,1,4,68,2]{4,3,2,1,0:T(8,128)}, u32[]{:S(2)}, u32[]{:S(2)}) collective-permute-start(f32[2,1,4,68,2]{4,3,2,1,0:T(8,128)} %get-tuple-element.91), channel_id=1, source_target_pairs={{1,0},{3,2},{5,4},{7,6},{9,8},{11,10},{13,12},{15,14},{17,16},{19,... | collective-permute-start | bytes 13064 | tf_op jit(solution)/shard_map/ppermute | solution.py:30
  102.0 86.0 %reduce-scatter.11.cloned.1.call-start = ((), (), s32[]{:S(2)}) async-start(), calls=%async_computation.17 | async-start | bytes 393216 | tf_op jit(solution)/shard_map/reduce_scatter | solution.py:211
  191.6 27.3 %all-to-all-start.1 = ((f32[64,1,512]{2,1,0:T(1,128)}), f32[64,1,512]{2,1,0:T(1,128)S(1)}, u32[]{:S(2)}, u32[]{:S(2)}) async-start(f32[64,1,512]{2,1,0:T(1,128)} %reshape.595), calls=%async_computation.3 | async-start | bytes 262144 | tf_op jit(solution)/shard_map/all_to_all | solution.py:214
  254.5 60.8 %reduce-scatter.13.cloned.1.call-start = ((), (), s32[]{:S(2)}) async-start(), calls=%async_computation.18 | async-start | bytes 393216 | tf_op jit(solution)/shard_map/reduce_scatter | solution.py:182
  265.5 33.6 %collective-permute-start.16 = (f32[2,1,4,68,2]{4,3,2,1,0:T(8,128)}, f32[2,1,4,68,2]{4,3,2,1,0:T(8,128)}, u32[]{:S(2)}, u32[]{:S(2)}) collective-permute-start(f32[2,1,4,68,2]{4,3,2,1,0:T(8,128)} %get-tuple-element.88), channel_id=1, source_target_pairs={{0,1},{2,3},{4,5},{6,7},{8,9},{10,11},{12,13},{14,15},{16,17},{18,... | collective-permute-start | bytes 13064 | tf_op jit(solution)/shard_map/ppermute | solution.py:28
  266.8 32.3 %collective-permute-start.17 = (f32[2,1,4,68,2]{4,3,2,1,0:T(8,128)}, f32[2,1,4,68,2]{4,3,2,1,0:T(8,128)}, u32[]{:S(2)}, u32[]{:S(2)}) collective-permute-start(f32[2,1,4,68,2]{4,3,2,1,0:T(8,128)} %get-tuple-element.89), channel_id=1, source_target_pairs={{1,0},{3,2},{5,4},{7,6},{9,8},{11,10},{13,12},{15,14},{17,16},{19,... | collective-permute-start | bytes 13064 | tf_op jit(solution)/shard_map/ppermute | solution.py:30
  297.4 63.6 %reduce-scatter.15.cloned.1.call-start = ((), (), s32[]{:S(2)}) async-start(), calls=%async_computation.19 | async-start | bytes 393216 | tf_op jit(solution)/shard_map/reduce_scatter | solution.py:211
  298.1 25.4 %collective-permute-start.9 = (f32[64,512]{1,0:T(8,128)}, f32[64,512]{1,0:T(8,128)}, u32[]{:S(2)}, u32[]{:S(2)}) collective-permute-start(f32[64,512]{1,0:T(8,128)} %slice_bitcast_fusion.19), channel_id=1, source_target_pairs={{0,128},{128,0},{1,129},{129,1},{2,130},{130,2},{3,131},{131,3},{4... | collective-permute-start | bytes 393224 | tf_op jit(solution)/shard_map/ppermute | solution.py:38
  364.6 24.7 %all-to-all-start.3 = ((f32[64,1,512]{2,1,0:T(1,128)}), f32[64,1,512]{2,1,0:T(1,128)}, u32[]{:S(2)}, u32[]{:S(2)}) async-start(f32[64,1,512]{2,1,0:T(1,128)} %reshape.599), calls=%async_computation.7 | async-start | bytes 262144 | tf_op jit(solution)/shard_map/all_to_all | solution.py:214
  429.3 60.8 %reduce-scatter.17.cloned.1.call-start = ((), (), s32[]{:S(2)}) async-start(), calls=%async_computation.20 | async-start | bytes 393216 | tf_op jit(solution)/shard_map/reduce_scatter | solution.py:182
  440.3 33.5 %collective-permute-start.25 = (f32[2,1,4,68,2]{4,3,2,1,0:T(8,128)}, f32[2,1,4,68,2]{4,3,2,1,0:T(8,128)}, u32[]{:S(2)}, u32[]{:S(2)}) collective-permute-start(f32[2,1,4,68,2]{4,3,2,1,0:T(8,128)} %get-tuple-element.86), channel_id=1, source_target_pairs={{0,1},{2,3},{4,5},{6,7},{8,9},{10,11},{12,13},{14,15},{16,17},{18,... | collective-permute-start | bytes 13064 | tf_op jit(solution)/shard_map/ppermute | solution.py:28
  441.6 32.2 %collective-permute-start.26 = (f32[2,1,4,68,2]{4,3,2,1,0:T(8,128)}, f32[2,1,4,68,2]{4,3,2,1,0:T(8,128)}, u32[]{:S(2)}, u32[]{:S(2)}) collective-permute-start(f32[2,1,4,68,2]{4,3,2,1,0:T(8,128)} %get-tuple-element.87), channel_id=1, source_target_pairs={{1,0},{3,2},{5,4},{7,6},{9,8},{11,10},{13,12},{15,14},{17,16},{19,... | collective-permute-start | bytes 13064 | tf_op jit(solution)/shard_map/ppermute | solution.py:30
  472.1 64.4 %reduce-scatter.19.cloned.1.call-start = ((), (), s32[]{:S(2)}) async-start(), calls=%async_computation.21 | async-start | bytes 393216 | tf_op jit(solution)/shard_map/reduce_scatter | solution.py:211
  472.8 26.2 %collective-permute-start.18 = (f32[64,512]{1,0:T(8,128)}, f32[64,512]{1,0:T(8,128)}, u32[]{:S(2)}, u32[]{:S(2)}) collective-permute-start(f32[64,512]{1,0:T(8,128)} %slice_bitcast_fusion.14), channel_id=1, source_target_pairs={{0,128},{128,0},{1,129},{129,1},{2,130},{130,2},{3,131},{131,3},{4... | collective-permute-start | bytes 393224 | tf_op jit(solution)/shard_map/ppermute | solution.py:38
  527.0 25.7 %collective-permute-start.31 = (f32[1,4,68,2]{3,2,1,0:T(8,128)}, f32[1,4,68,2]{3,2,1,0:T(8,128)}, u32[]{:S(2)}, u32[]{:S(2)}) collective-permute-start(f32[1,4,68,2]{3,2,1,0:T(8,128)} %get-tuple-element.103), channel_id=1, source_target_pairs={{0,1},{2,3},{4,5},{6,7},{8,9},{10,11},{12,13},{14,15},{16,17},{18,... | collective-permute-start | bytes 6536 | tf_op jit(solution)/shard_map/ppermute | solution.py:28
  540.1 24.5 %all-to-all-start.5 = ((f32[64,1,512]{2,1,0:T(1,128)}), f32[64,1,512]{2,1,0:T(1,128)}, u32[]{:S(2)}, u32[]{:S(2)}) async-start(f32[64,1,512]{2,1,0:T(1,128)} %reshape.603), calls=%async_computation.11 | async-start | bytes 262144 | tf_op jit(solution)/shard_map/all_to_all | solution.py:214
  600.6 51.9 %reduce-scatter.21.cloned.1.call-start = ((), (), s32[]{:S(2)}) async-start(), calls=%async_computation.22 | async-start | bytes 393216 | tf_op jit(solution)/shard_map/reduce_scatter | solution.py:182
  637.2 49.6 %reduce-scatter.23.cloned.1.call-start = ((), (), s32[]{:S(2)}) async-start(), calls=%async_computation.23 | async-start | bytes 393216 | tf_op jit(solution)/shard_map/reduce_scatter | solution.py:211
  645.3 25.3 %collective-permute-start.34 = (f32[2,1,4,68,2]{4,3,2,1,0:T(8,128)}, f32[2,1,4,68,2]{4,3,2,1,0:T(8,128)S(1)}, u32[]{:S(2)}, u32[]{:S(2)}) collective-permute-start(f32[2,1,4,68,2]{4,3,2,1,0:T(8,128)} %get-tuple-element.84), channel_id=1, source_target_pairs={{0,1},{2,3},{4,5},{6,7},{8,9},{10,11},{12,13},{14,15},{16,17},{18,... | collective-permute-start | bytes 13064 | tf_op jit(solution)/shard_map/ppermute | solution.py:28
  688.8 24.6 %all-to-all-start.7 = ((f32[64,1,512]{2,1,0:T(1,128)}), f32[64,1,512]{2,1,0:T(1,128)S(1)}, u32[]{:S(2)}, u32[]{:S(2)}) async-start(f32[64,1,512]{2,1,0:T(1,128)} %reshape.607), calls=%async_computation.15 | async-start | bytes 262144 | tf_op jit(solution)/shard_map/all_to_all | solution.py:214
  (81 other events, 1213.0 us)
Sparse Core Ops, SparseCore 0:
  102.1 28.2 reduce-scatter.8
  169.9 18.0 reduce-scatter.10
  297.5 17.7 reduce-scatter.12
  342.8 18.0 reduce-scatter.14
  472.2 17.8 reduce-scatter.16
  518.4 18.0 reduce-scatter.18
  637.3 8.9 reduce-scatter.20
  670.7 16.0 reduce-scatter.22
